TPU v7x, 256 devices: a whole 4x4x8 slice. The times are simulated.
256 devices in a mesh: row: 8 (over x, z_lo), col: 32 (over y, z_hi, core).
Axes of the slice: x: 4, y: 4, z: 8 (z_hi: 4, z_lo: 2; z = z_hi * 2 + z_lo), core: 2. Of those that a mesh axis runs over, the one named last changes fastest.
Arguments:
- hamiltonian: float32 [4096, 4096], P('row', 'col'), as said below
- h_mask: int32 [32, 32], P('row', 'col'), may hold values from 0 to 1, as said below
- factor: float32 [4096, 4096], P('row', 'col'), may hold values from -0.125 to 0.125
- z_mask: int32 [32, 32], P('row', 'col'), may hold values 0 or 1
- k_mask: int32 [32, 32], P('row', 'col'), may hold values 0 or 1
- block_sizes: int32 [32], replicated, may hold values from 64 to 128, as said below
Outputs:
- transformed: float32 [4096, 4096], P('row', 'col')
Inputs may be any that keep to these rules, and one draw needn't show every extreme that they name: hamiltonian is symmetric. `h_mask`: symmetric, with every diagonal block occupied. `block_sizes`: some block uses all 128 orbitals.
All inputs are finite; a program needn't handle non-finite values. No bound on the sum of `z_mask` or of `k_mask` on one device may be relied on, other than what follows from the above.
Results may differ from a plain program's by a relative error of at most 0.000098.
Values sent between devices are 32-bit elements; how exact they have to be, the bound alone decides.
A program may use at most 64 MiB of HBM per device.

v0:
```python
import jax
import jax.numpy as jnp
from jax import lax
from jax.sharding import PartitionSpec as P

BLOCK = 128


def expand(blocks):
    grown = jnp.repeat(blocks.astype(jnp.float32), BLOCK, axis=0)
    return jnp.repeat(grown, BLOCK, axis=1)


def validity(block_sizes, first, count):
    sizes = lax.dynamic_slice_in_dim(block_sizes, first, count, 0)
    within = jnp.arange(BLOCK, dtype=jnp.int32)
    return (within[None, :] < sizes[:, None]).astype(jnp.float32).reshape(-1)


def local(hamiltonian, h_mask, factor, z_mask, k_mask, block_sizes):
    rows_here, cols_here = hamiltonian.shape
    row_blocks = rows_here // BLOCK
    col_blocks = cols_here // BLOCK
    row_place = lax.axis_index("row")
    row_first = row_place * row_blocks
    col_first = lax.axis_index("col") * col_blocks
    row_valid = validity(block_sizes, row_first, row_blocks)
    col_valid = validity(block_sizes, col_first, col_blocks)
    outer = row_valid[:, None] * col_valid[None, :]
    global_rows = row_first * BLOCK + jnp.arange(rows_here, dtype=jnp.int32)
    global_cols = col_first * BLOCK + jnp.arange(cols_here, dtype=jnp.int32)
    upper = (global_rows[:, None] <= global_cols[None, :]).astype(jnp.float32)
    hmat = hamiltonian * expand(h_mask) * outer
    zmat = factor * expand(z_mask) * outer * upper
    highest = lax.Precision.HIGHEST
    zcolumn = lax.all_gather(zmat, "row", axis=0, tiled=True)
    hz_tile = jnp.dot(
        lax.all_gather(hmat, "col", axis=1, tiled=True),
        zcolumn,
        precision=highest,
        preferred_element_type=jnp.float32,
    )
    terms = jnp.dot(
        lax.all_gather(zmat, "col", axis=1, tiled=True).T,
        hz_tile,
        precision=highest,
        preferred_element_type=jnp.float32,
    )
    result = lax.psum_scatter(terms, "row", scatter_dimension=0, tiled=True)
    return result * expand(k_mask)


def solution(mesh):
    placed = (
        P("row", "col"),
        P("row", "col"),
        P("row", "col"),
        P("row", "col"),
        P("row", "col"),
        P(),
    )
    return jax.shard_map(
        local, mesh=mesh, in_specs=placed, out_specs=P("row", "col"), check_vma=False
    )
```

profile of v0, /device:TPU:1, one launch (start us, length us, event | category | flops | bytes accessed | tf_op | source)
XLA Modules:
  0.0 323.2 jit_solution(6343206805627346707)
XLA Ops:
  6.5 0.0 all-gather.8.cloned.1.call-start
  6.5 0.7 dynamic_slice.6
  7.3 0.1 convert_bitcast_fusion
  7.3 1.2 dynamic_slice.7
  8.6 0.6 compare_convert_fusion
  9.3 0.7 convert_bitcast_fusion.2
  9.9 0.7 convert_bitcast_fusion.3
  10.6 0.1 broadcast_bitcast_fusion.1
  10.7 2.1 multiply_multiply_fusion
  12.8 0.0 all-gather.8.cloned.1.call-update
  12.8 0.0 all-gather.6.cloned.1.call-start
  12.9 0.7 all-gather.6.cloned.1.call-update
  13.6 0.0 all-gather.4.cloned.1.call-start
  13.6 0.7 all-gather.4.cloned.1.call-update
  14.3 0.0 reduce-scatter.2.cloned.1.call-start
  14.3 56.9 %all-gather.8.cloned.1.call-done = f32[4096,128]{1,0:T(8,128)} async-done(((f32[512,128]{1,0:T(8,128)}), f32[4096,128]{1,0:T(8,128)}) %all-gather.8.cloned.1.call-update) | async-done | bytes 2097168 | tf_op jit(solution)/shard_map/all_gather | solution.py:36
  71.2 88.0 %all-gather.6.cloned.1.call-done = f32[512,4096]{1,0:T(8,128)} async-done(((f32[512,128]{1,0:T(8,128)}), f32[512,4096]{1,0:T(8,128)}) %all-gather.6.cloned.1.call-update) | async-done | bytes 8388624 | tf_op jit(solution)/shard_map/all_gather | solution.py:38
  159.3 9.3 %fusion.1 = f32[512,128]{1,0:T(8,128)S(1)} fusion(f32[512,4096]{1,0:T(8,128)} %all-gather.6.cloned.1.call-done, f32[4096,128]{1,0:T(8,128)} %all-gather.8.cloned.1.call-done), kind=kOutput, calls=%fused_computation.15 | convolution fusion | flops 3221225472 | bytes 10747904 | tf_op jit(solution)/shard_map/dot_general | solution.py:37
  168.6 0.0 copy-start
  168.6 76.9 %all-gather.4.cloned.1.call-done = f32[512,4096]{1,0:T(8,128)} async-done(((f32[512,128]{1,0:T(8,128)}), f32[512,4096]{1,0:T(8,128)}) %all-gather.4.cloned.1.call-update) | async-done | bytes 8388624 | tf_op jit(solution)/shard_map/all_gather | solution.py:44
  245.6 16.5 %fusion.2 = f32[4096,128]{1,0:T(8,128)} fusion(f32[512,4096]{1,0:T(8,128)} %all-gather.4.cloned.1.call-done, f32[512,128]{1,0:T(8,128)S(1)} %fusion.1), kind=kOutput, calls=%fused_computation.16 | convolution fusion | flops 3221225472 | bytes 10747904 | tf_op jit(solution)/shard_map/dot_general | solution.py:43
  262.1 0.0 reduce-scatter.2.cloned.1.call-update
  262.1 0.0 copy-done
  262.1 0.1 broadcast_bitcast_fusion
  262.2 52.7 %reduce-scatter.2.cloned.1.call-done = f32[512,128]{1,0:T(8,128)} async-done(((f32[4096,128]{1,0:T(8,128)}), f32[512,128]{1,0:T(8,128)}) %reduce-scatter.2.cloned.1.call-update) | async-done | bytes 262160 | tf_op jit(solution)/shard_map/reduce_scatter | solution.py:49
  314.9 1.8 broadcast_multiply_fusion
  (3 shorter events, 0.0 us)
Async XLA Ops:
  6.5 64.7 %all-gather.8.cloned.1.call-start = ((), (), s32[]{:S(2)}) async-start(), calls=%async_computation.3 | async-start | bytes 2359296 | tf_op jit(solution)/shard_map/all_gather | solution.py:36
  12.8 146.4 %all-gather.6.cloned.1.call-start = ((), (), s32[]{:S(2)}) async-start(), calls=%async_computation.2 | async-start | bytes 8650752 | tf_op jit(solution)/shard_map/all_gather | solution.py:38
  13.6 232.0 %all-gather.4.cloned.1.call-start = ((), (), s32[]{:S(2)}) async-start(), calls=%async_computation.1 | async-start | bytes 8650752 | tf_op jit(solution)/shard_map/all_gather | solution.py:44
  14.3 300.6 %reduce-scatter.2.cloned.1.call-start = ((), (), s32[]{:S(2)}) async-start(), calls=%async_computation.4 | async-start | bytes 2359296 | tf_op jit(solution)/shard_map/reduce_scatter | solution.py:49
  168.6 93.5 %copy-start = (s32[4,1]{0,1:T(1,128)S(1)}, s32[4,1]{0,1:T(1,128)}, u32[]{:S(2)}) copy-start(s32[4,1]{0,1:T(1,128)} %param.10) | copy-start | bytes 52
Sparse Core Ops, SparseCore 0:
  12.9 58.2 all-gather.7
  73.7 85.4 all-gather.5
  161.7 83.7 all-gather.3
  262.2 52.6 reduce-scatter.1
where the time goes:
time: 323 us
  waiting for transfers between devices  276 us (85%)
  matrix products  25.9 us (8%)
  between operations  13.2 us (4%)
  other arithmetic  5.97 us (2%)
    all_gather x1, waiting for transfers between devices, local(): lax.all_gather(hmat, 'col', axis=1, tiled=True)  88 us
    all_gather x1, waiting for transfers between devices, local(): lax.all_gather(zmat, 'col', axis=1, tiled=True)  76.9 us
    all_gather x1, waiting for transfers between devices, local(): zcolumn = lax.all_gather(zmat, 'row', axis=0, tiled=True)  56.9 us
    reduce_scatter x1, waiting for transfers between devices, local(): result = lax.psum_scatter(terms, 'row', scatter_dimension=0, tiled=True)  52.7 us
    dot_general x1, matrix products, local(): jnp.dot(lax.all_gather(zmat, 'col', axis=1, tiled=True).T, hz_tile, preci...  16.5 us
    dot_general x1, matrix products, local(): jnp.dot(lax.all_gather(hmat, 'col', axis=1, tiled=True), zcolumn, precisi...  9.35 us
  transfers between devices with their start and end apart: 4, of which 4 were waited for; matrix products, arithmetic and copies ran while one was open for 3% of the time, Pallas kernels for 0%

commit v1 on v0

--- a/solution.py
+++ b/solution.py
@@ -35,7 +35,9 @@
     highest = lax.Precision.HIGHEST
     zcolumn = lax.all_gather(zmat, "row", axis=0, tiled=True)
     hz_tile = jnp.dot(
-        lax.all_gather(hmat, "col", axis=1, tiled=True),
+        jnp.concatenate(
+            lax.all_to_all(jnp.stack([hmat] * lax.axis_size("col")), "col", 0, 0), axis=1
+        ),
         zcolumn,
         precision=highest,
         preferred_element_type=jnp.float32,

time: 323 us -> 398 us (1.23)
  waiting for transfers between devices: 276 us -> 327 us
  starting transfers between devices: 0.12 us -> 12.9 us
  matrix products: 25.9 us -> 32.3 us
  local copies, waits for them, and re-layouts: 2.11 us -> 6.53 us
    all_to_all x0 -> x1, waiting for transfers between devices: none -> 89.6 us  [local(): lax.all_to_all(jnp.stack([hmat] * lax.axis_size('col')), 'col', 0, 0)]
    all_gather x1 -> x0, waiting for transfers between devices: 88 us -> none  [local(): lax.all_gather(hmat, 'col', axis=1, tiled=True)]
    all_gather x1, waiting for transfers between devices: 56.9 us -> 137 us  [local(): zcolumn = lax.all_gather(zmat, 'row', axis=0, tiled=True)]
    all_gather x1, waiting for transfers between devices: 76.9 us -> 47.8 us  [local(): lax.all_gather(zmat, 'col', axis=1, tiled=True)]
    all_to_all x0 -> x1, starting transfers between devices: none -> 12.8 us  [local(): lax.all_to_all(jnp.stack([hmat] * lax.axis_size('col')), 'col', 0, 0)]
    dot_general x1, matrix products: 9.35 us -> 15.8 us  [local(): jnp.dot(jnp.concatenate(lax.all_to_all(jnp.stack([hmat] * lax.axis_size('...]
    another operation x0 -> x1, local copies, waits for them, and re-layouts: none -> 4.29 us  [local(): jnp.stack([hmat] * lax.axis_size('col'))]
  transfers between devices with their start and end apart: 4 -> 4, of which waited for: 4 -> 4; matrix products, arithmetic and copies ran while one was open for 3% -> 5% of each run, Pallas kernels for 0% -> 0%
where the time goes in v1:
time: 398 us
  waiting for transfers between devices  327 us (82%)
  matrix products  32.3 us (8%)
  between operations  13.2 us (3%)
  starting transfers between devices  12.9 us (3%)
  local copies, waits for them, and re-layouts  6.53 us (2%)
  other arithmetic  5.9 us (1%)
    all_gather x1, waiting for transfers between devices, local(): zcolumn = lax.all_gather(zmat, 'row', axis=0, tiled=True)  137 us
    all_to_all x1, waiting for transfers between devices, local(): lax.all_to_all(jnp.stack([hmat] * lax.axis_size('col')), 'col', 0, 0)  89.6 us
    reduce_scatter x1, waiting for transfers between devices, local(): result = lax.psum_scatter(terms, 'row', scatter_dimension=0, tiled=True)  52.7 us
    all_gather x1, waiting for transfers between devices, local(): lax.all_gather(zmat, 'col', axis=1, tiled=True)  47.8 us
    dot_general x1, matrix products, local(): jnp.dot(lax.all_gather(zmat, 'col', axis=1, tiled=True).T, hz_tile, preci...  16.5 us
    dot_general x1, matrix products, local(): jnp.dot(jnp.concatenate(lax.all_to_all(jnp.stack([hmat] * lax.axis_size('...  15.8 us
    all_to_all x1, starting transfers between devices, local(): lax.all_to_all(jnp.stack([hmat] * lax.axis_size('col')), 'col', 0, 0)  12.8 us
  transfers between devices with their start and end apart: 4, of which 4 were waited for; matrix products, arithmetic and copies ran while one was open for 5% of the time, Pallas kernels for 0%

profile of v1, /device:TPU:1, one launch (start us, length us, event | category | flops | bytes accessed | tf_op | source)
XLA Modules:
  0.0 398.3 jit_solution(17732666167369030107)
XLA Ops:
  6.5 0.0 all-gather.5.cloned.1.call-start
  6.5 0.7 dynamic_slice.6
  7.3 0.1 convert_bitcast_fusion
  7.3 1.2 dynamic_slice.7
  8.6 0.6 compare_convert_fusion
  9.3 0.7 convert_bitcast_fusion.2
  9.9 0.7 convert_bitcast_fusion.3
  10.6 0.1 broadcast_bitcast_fusion.1
  10.7 2.1 multiply_multiply_fusion
  12.7 0.0 all-gather.5.cloned.1.call-update
  12.7 0.1 copy.7
  12.9 4.3 %stack.2 = f32[32,512,128]{1,2,0:T(8,128)} broadcast(f32[512,128]{0,1:T(8,128)S(1)} %copy.7), dimensions={1,2} | broadcast | bytes 8650752 | tf_op jit(solution)/shard_map/stack | solution.py:39
  17.2 12.8 %all-to-all-start = ((f32[32,512,128]{1,2,0:T(8,128)}), f32[32,512,128]{1,2,0:T(8,128)}, u32[]{:S(2)}, u32[]{:S(2)}) async-start(f32[32,512,128]{1,2,0:T(8,128)} %stack.2), calls=%async_computation | async-start | bytes 16777216 | tf_op jit(solution)/shard_map/all_to_all | solution.py:39
  30.0 0.0 all-gather.3.cloned.1.call-start
  30.0 0.7 all-gather.3.cloned.1.call-update
  30.7 0.0 reduce-scatter.2.cloned.1.call-start
  30.8 136.5 %all-gather.5.cloned.1.call-done = f32[4096,128]{1,0:T(8,128)} async-done(((f32[512,128]{1,0:T(8,128)}), f32[4096,128]{1,0:T(8,128)}) %all-gather.5.cloned.1.call-update) | async-done | bytes 2097168 | tf_op jit(solution)/shard_map/all_gather | solution.py:36
  167.3 89.6 %all-to-all-done = f32[32,512,128]{1,2,0:T(8,128)} async-done(((f32[32,512,128]{1,2,0:T(8,128)}), f32[32,512,128]{1,2,0:T(8,128)}, u32[]{:S(2)}, u32[]{:S(2)}) %all-to-all-start) | async-done | bytes 8388640 | tf_op jit(solution)/shard_map/all_to_all | solution.py:39
  256.9 15.8 %fusion.1 = f32[512,128]{1,0:T(8,128)S(1)} fusion(f32[512,4096]{0,1:T(8,128)} %bitcast.7, f32[4096,128]{1,0:T(8,128)} %all-gather.5.cloned.1.call-done), kind=kOutput, calls=%fused_computation.15 | convolution fusion | flops 3221225472 | bytes 10747904 | tf_op jit(solution)/shard_map/dot_general | solution.py:37
  272.8 0.0 copy-start
  272.8 47.8 %all-gather.3.cloned.1.call-done = f32[512,4096]{1,0:T(8,128)} async-done(((f32[512,128]{1,0:T(8,128)}), f32[512,4096]{1,0:T(8,128)}) %all-gather.3.cloned.1.call-update) | async-done | bytes 8388624 | tf_op jit(solution)/shard_map/all_gather | solution.py:46
  320.6 16.5 %fusion.2 = f32[4096,128]{1,0:T(8,128)} fusion(f32[512,4096]{1,0:T(8,128)} %all-gather.3.cloned.1.call-done, f32[512,128]{1,0:T(8,128)S(1)} %fusion.1), kind=kOutput, calls=%fused_computation.16 | convolution fusion | flops 3221225472 | bytes 10747904 | tf_op jit(solution)/shard_map/dot_general | solution.py:45
  337.1 0.0 reduce-scatter.2.cloned.1.call-update
  337.2 0.0 copy-done
  337.2 0.1 broadcast_bitcast_fusion
  337.2 52.7 %reduce-scatter.2.cloned.1.call-done = f32[512,128]{1,0:T(8,128)} async-done(((f32[4096,128]{1,0:T(8,128)}), f32[512,128]{1,0:T(8,128)}) %reduce-scatter.2.cloned.1.call-update) | async-done | bytes 262160 | tf_op jit(solution)/shard_map/reduce_scatter | solution.py:51
  389.9 1.8 broadcast_multiply_fusion
  (3 shorter events, 0.0 us)
Async XLA Ops:
  6.5 160.8 %all-gather.5.cloned.1.call-start = ((), (), s32[]{:S(2)}) async-start(), calls=%async_computation.3 | async-start | bytes 2359296 | tf_op jit(solution)/shard_map/all_gather | solution.py:36
  17.2 239.7 %all-to-all-start = ((f32[32,512,128]{1,2,0:T(8,128)}), f32[32,512,128]{1,2,0:T(8,128)}, u32[]{:S(2)}, u32[]{:S(2)}) async-start(f32[32,512,128]{1,2,0:T(8,128)} %stack.2), calls=%async_computation | async-start | bytes 16777216 | tf_op jit(solution)/shard_map/all_to_all | solution.py:39
  30.0 290.6 %all-gather.3.cloned.1.call-start = ((), (), s32[]{:S(2)}) async-start(), calls=%async_computation.2 | async-start | bytes 8650752 | tf_op jit(solution)/shard_map/all_gather | solution.py:46
  30.7 359.2 %reduce-scatter.2.cloned.1.call-start = ((), (), s32[]{:S(2)}) async-start(), calls=%async_computation.4 | async-start | bytes 2359296 | tf_op jit(solution)/shard_map/reduce_scatter | solution.py:51
  272.8 64.4 %copy-start = (s32[4,1]{0,1:T(1,128)S(1)}, s32[4,1]{0,1:T(1,128)}, u32[]{:S(2)}) copy-start(s32[4,1]{0,1:T(1,128)} %param.10) | copy-start | bytes 52
Sparse Core Ops, SparseCore 0:
  12.9 154.4 all-gather.4
  169.8 150.7 all-gather.2
  337.3 52.6 reduce-scatter.1
